TPU v7x, 32 devices: a whole 2x2x4 slice. The times are simulated.
32 devices in a mesh: term: 8 (over y, x, core), topic: 4 (over z).
Axes of the slice: x: 2, y: 2, z: 4, core: 2. Of those that a mesh axis runs over, the one named last changes fastest.
Arguments:
- factor: bfloat16 [65536, 512], P('term', 'topic'), may hold values from 1e-06 to 0.05, as said below
- tile_values: bfloat16 [65536, 128], P('term'), may hold values from 0.049804688 to 1
- tile_docs: int32 [8, 128], P('term'), may hold values from 0 to 127, as said below
- codes: float32 [512, 128], P('topic', 'term'), may hold values from 0.1 to 2
- gram_stat: float32 [512, 512], P('topic', 'term'), may hold values from 0 to 4
- data_stat: float32 [65536, 512], P('term', 'topic'), may hold values from 0 to 0.4
Outputs:
- codes_out: float32 [512, 128], P('topic', 'term')
- gram_new: float32 [512, 512], P('topic', 'term')
- data_new: float32 [65536, 512], P('term', 'topic')
Inputs may be any that keep to these rules, and one draw needn't show every extreme that they name: `tile_docs`: each row lists 128 different document numbers. `factor`: positive entries.
All inputs are finite; a program needn't handle non-finite values.
Results may differ from a plain program's by a relative error of at most 0.0003.
Values may be sent and summed in bfloat16 or wider, within the bound.
No kernel may reach another device: no remote copies, remote signals or barrier semaphores. Data moves between devices by JAX's collectives and lax.ppermute only.
A program may use at most 128 MiB of HBM per device.

v0:
```python
import jax
import jax.numpy as jnp
from jax import lax
from jax.sharding import PartitionSpec as P

ITERS = 3
EPSILON = 1e-06
DECAY = 0.5


def contract_rows(left, right):
    return lax.dot_general(
        left, right, (((0,), (0,)), ((), ())), preferred_element_type=jnp.float32
    )


def apply_gram(gram_rows, current):
    return jnp.dot(
        gram_rows,
        lax.all_gather(current, "topic", axis=0, tiled=True),
        precision=lax.Precision.HIGHEST,
        preferred_element_type=jnp.float32,
    )


def per_device(factor, tile_values, tile_docs, codes, gram_stat, data_stat):
    term_count = lax.axis_size("term")
    documents = codes.shape[1] * term_count
    onehot = (tile_docs[0][:, None] == jnp.arange(documents, dtype=jnp.int32)[None, :]).astype(
        jnp.bfloat16
    )
    batch = jnp.dot(tile_values, onehot, preferred_element_type=jnp.float32).astype(jnp.bfloat16)
    partial_data = contract_rows(factor, batch)
    data_share = lax.psum_scatter(partial_data, "term", scatter_dimension=1, tiled=True)
    row_block = lax.all_to_all(factor, "topic", split_axis=0, concat_axis=1, tiled=True)
    gram_part = lax.psum_scatter(
        contract_rows(row_block, row_block), "topic", scatter_dimension=0, tiled=True
    )
    gram_rows = lax.psum(gram_part, "term")
    current = codes
    for update in range(ITERS):
        current = current * data_share / (apply_gram(gram_rows, current) + EPSILON)
    outer = lax.dot_general(
        current,
        lax.all_gather(current, "topic", axis=0, tiled=True),
        (((1,), (1,)), ((), ())),
        precision=lax.Precision.HIGHEST,
        preferred_element_type=jnp.float32,
    )
    outer_share = lax.psum_scatter(outer, "term", scatter_dimension=1, tiled=True)
    gram_new = DECAY * gram_stat + outer_share / documents
    code_row = lax.all_gather(current, "term", axis=1, tiled=True)
    widened = batch.astype(jnp.float32)
    product = lax.dot_general(
        widened,
        code_row,
        (((1,), (1,)), ((), ())),
        precision=lax.Precision.HIGHEST,
        preferred_element_type=jnp.float32,
    )
    data_new = DECAY * data_stat + product / documents
    return (current, gram_new, data_new)


def solution(mesh):
    placed = (
        P("term", "topic"),
        P("term", None),
        P("term", None),
        P("topic", "term"),
        P("topic", "term"),
        P("term", "topic"),
    )
    return jax.shard_map(
        per_device,
        mesh=mesh,
        in_specs=placed,
        out_specs=(P("topic", "term"), P("topic", "term"), P("term", "topic")),
        check_vma=False,
    )
```

profile of v0, /device:TPU:0, one launch (start us, length us, event | category | flops | bytes accessed | tf_op | source)
XLA Modules:
  0.0 284.7 jit_solution(639582228280729309)
XLA Ops:
  7.2 0.0 copy-start
  7.2 0.0 reduce-scatter.6.cloned.1.call-start
  7.2 54.8 %all_to_all.19 = bf16[4,2048,128]{2,1,0:T(8,128)(2,1)} all-to-all(bf16[4,2048,128]{2,1,0:T(8,128)(2,1)} %bitcast.21), channel_id=1, replica_groups=mesh['term'=8,'topic'=4] {'topic'}, dimensions={0} | all-to-all | bytes 4194304 | tf_op jit(solution)/shard_map/all_to_all | solution.py:35
  62.0 3.9 %copy.9 = bf16[2048,4,128]{0,2,1:T(8,128)(2,1)} copy(bf16[2048,4,128]{2,0,1:T(8,128)(2,1)} %bitcast.22) | data formatting | bytes 4194304 | tf_op jit(solution)/shard_map/all_to_all | solution.py:35
  66.0 0.0 copy-start.6
  66.0 4.5 %fusion.7 = f32[512,512]{1,0:T(8,128)} fusion(bf16[2048,512]{0,1:T(8,128)(2,1)} %bitcast.23), kind=kOutput, calls=%fused_computation.14 | convolution fusion | flops 1073741824 | bytes 3145728 | tf_op jit(solution)/shard_map/dot_general | solution.py:12
  70.5 0.0 reduce-scatter.6.cloned.1.call-update
  70.5 0.0 reduce-scatter.4.cloned.1.call-start
  70.5 0.0 copy-done
  70.5 0.0 copy-done.6
  70.6 0.0 copy-start.2
  70.6 0.8 convolution_convert_fusion
  71.4 0.0 copy-start.1
  71.4 1.3 copy-done.1
  72.7 0.0 copy-done.2
  72.7 0.0 copy-start.5
  72.7 1.3 convolution_bitcast_fusion
  74.1 0.0 reduce-scatter.4.cloned.1.call-update
  74.1 0.0 all-reduce.2.cloned.1.call-start
  74.1 23.0 %reduce-scatter.6.cloned.1.call-done = f32[128,512]{1,0:T(8,128)} async-done(((f32[512,512]{1,0:T(8,128)}), f32[128,512]{1,0:T(8,128)}) %reduce-scatter.6.cloned.1.call-update) | async-done | bytes 262160 | tf_op jit(solution)/shard_map/reduce_scatter | solution.py:36
  97.2 0.0 all-reduce.2.cloned.1.call-update
  97.2 0.0 reduce-scatter.8.cloned.1.call-start
  97.2 0.0 copy-done.5
  97.3 13.1 %all_gather.15 = f32[512,16]{0,1:T(8,128)S(1)} all-gather(f32[128,16]{0,1:T(8,128)S(1)} %copy-done.5), channel_id=1, replica_groups=mesh['term'=8,'topic'=4] {'topic'}, dimensions={0}, use_global_device_ids=true | all-gather | bytes 40960 | tf_op jit(solution)/shard_map/all_gather | solution.py:20
  110.4 22.4 %reduce-scatter.4.cloned.1.call-done = f32[128,16]{0,1:T(8,128)} async-done(((f32[128,128]{0,1:T(8,128)}), f32[128,16]{0,1:T(8,128)}) %reduce-scatter.4.cloned.1.call-update) | async-done | bytes 8208 | tf_op jit(solution)/shard_map/reduce_scatter | solution.py:34
  132.8 57.0 %all-reduce.2.cloned.1.call-done = f32[128,512]{1,0:T(8,128)} async-done(((f32[128,512]{1,0:T(8,128)}), f32[128,512]{1,0:T(8,128)}) %all-reduce.2.cloned.1.call-update) | async-done | bytes 262160 | tf_op jit(solution)/shard_map/psum | solution.py:39
  189.8 1.3 fusion.3
  191.0 13.2 %all_gather.16 = f32[512,16]{0,1:T(8,128)S(1)} all-gather(f32[128,16]{0,1:T(8,128)S(1)} %fusion.3), channel_id=1, replica_groups=mesh['term'=8,'topic'=4] {'topic'}, dimensions={0}, use_global_device_ids=true | all-gather | bytes 40960 | tf_op jit(solution)/shard_map/all_gather | solution.py:20
  204.2 1.3 fusion.2
  205.5 13.1 %all_gather.17 = f32[512,16]{0,1:T(8,128)S(1)} all-gather(f32[128,16]{0,1:T(8,128)S(1)} %fusion.2), channel_id=1, replica_groups=mesh['term'=8,'topic'=4] {'topic'}, dimensions={0}, use_global_device_ids=true | all-gather | bytes 40960 | tf_op jit(solution)/shard_map/all_gather | solution.py:20
  218.6 1.3 fusion.1
  219.9 0.0 copy-start.3
  219.9 8.6 %all_gather.19 = f32[128,128]{0,1:T(8,128)S(1)} all-gather(f32[128,16]{0,1:T(8,128)S(1)} %fusion.1), channel_id=1, replica_groups=mesh['term'=8,'topic'=4] {'term'}, dimensions={1}, use_global_device_ids=true | all-gather | bytes 73728 | tf_op jit(solution)/shard_map/all_gather | solution.py:52
  228.6 13.1 %all_gather.18 = f32[512,16]{0,1:T(8,128)S(1)} all-gather(f32[128,16]{0,1:T(8,128)S(1)} %fusion.1), channel_id=1, replica_groups=mesh['term'=8,'topic'=4] {'topic'}, dimensions={0}, use_global_device_ids=true | all-gather | bytes 40960 | tf_op jit(solution)/shard_map/all_gather | solution.py:45
  241.7 1.3 fusion.8
  243.0 0.0 reduce-scatter.8.cloned.1.call-update
  243.0 0.0 copy-start.4
  243.0 7.4 %fusion = f32[8192,128]{1,0:T(8,128)} fusion(bf16[128,8192]{1,0:T(8,128)(2,1)} %copy-done.1, f32[128,128]{0,1:T(8,128)S(1)} %all_gather.19, f32[8192,128]{1,0:T(8,128)} %param.11), kind=kOutput, calls=%fused_computation.1 | convolution fusion | flops 1613758464 | bytes 10551296 | tf_op jit(solution)/shard_map/dot_general | solution.py:54
  250.4 0.0 copy-done.3
  250.4 26.5 %reduce-scatter.8.cloned.1.call-done = f32[128,64]{0,1:T(8,128)} async-done(((f32[128,512]{0,1:T(8,128)}), f32[128,64]{0,1:T(8,128)}) %reduce-scatter.8.cloned.1.call-update) | async-done | bytes 32784 | tf_op jit(solution)/shard_map/reduce_scatter | solution.py:50
  276.8 0.0 copy-done.4
  276.8 1.4 multiply_add_fusion
Async XLA Ops:
  7.2 63.4 %copy-start = (bf16[8192,128]{1,0:T(8,128)(2,1)S(1)}, bf16[8192,128]{1,0:T(8,128)(2,1)}, u32[]{:S(2)}) copy-start(bf16[8192,128]{1,0:T(8,128)(2,1)} %param.7) | copy-start | bytes 6291460
  7.2 90.0 %reduce-scatter.6.cloned.1.call-start = ((), (), s32[]{:S(2)}) async-start(), calls=%async_computation.5 | async-start | bytes 1310720 | tf_op jit(solution)/shard_map/reduce_scatter | solution.py:36
  66.0 4.6 %copy-start.6 = (s32[1,128]{1,0:T(1,128)S(1)}, s32[1,128]{1,0:T(1,128)}, u32[]{:S(2)}) copy-start(s32[1,128]{1,0:T(1,128)} %param.8) | copy-start | bytes 1540
  70.5 62.3 %reduce-scatter.4.cloned.1.call-start = ((), (), s32[]{:S(2)}) async-start(), calls=%async_computation.4 | async-start | bytes 73728 | tf_op jit(solution)/shard_map/reduce_scatter | solution.py:34
  70.6 2.2 copy-start.2
  71.4 1.3 copy-start.1
  72.7 24.5 %copy-start.5 = (f32[128,16]{0,1:T(8,128)S(1)}, f32[128,16]{0,1:T(8,128)}, u32[]{:S(2)}) copy-start(f32[128,16]{0,1:T(8,128)} %param.9) | copy-start | bytes 24580
  74.1 115.7 %all-reduce.2.cloned.1.call-start = ((), (), s32[]{:S(2)}) async-start(), calls=%async_computation.6 | async-start | bytes 524288 | tf_op jit(solution)/shard_map/psum | solution.py:39
  97.2 179.6 %reduce-scatter.8.cloned.1.call-start = ((), (), s32[]{:S(2)}) async-start(), calls=%async_computation.7 | async-start | bytes 294912 | tf_op jit(solution)/shard_map/reduce_scatter | solution.py:50
  219.9 30.4 %copy-start.3 = (f32[128,16]{0,1:T(8,128)}, f32[128,16]{0,1:T(8,128)S(1)}, u32[]{:S(2)}) copy-start(f32[128,16]{0,1:T(8,128)S(1)} %fusion.1) | copy-start | bytes 24580
  243.0 33.8 %copy-start.4 = (f32[128,64]{0,1:T(8,128)S(1)}, f32[128,64]{0,1:T(8,128)}, u32[]{:S(2)}) copy-start(f32[128,64]{0,1:T(8,128)} %param.10) | copy-start | bytes 98308
Sparse Core Ops, SparseCore 0:
  70.6 26.5 reduce-scatter.5
  100.7 31.9 reduce-scatter.3
  135.8 53.8 all-reduce.1
  243.1 33.6 reduce-scatter.7
where the time goes:
time: 285 us
  waiting for transfers between devices  129 us (45%)
  blocking collectives  116 us (41%)
  matrix products  19.1 us (7%)
  between operations  13.9 us (5%)
  local copies, waits for them, and re-layouts  5.32 us (2%)
    psum x1, waiting for transfers between devices, per_device(): gram_rows = lax.psum(gram_part, 'term')  57 us
    all_to_all x1, blocking collectives, per_device(): lax.all_to_all(factor, 'topic', split_axis=0, concat_axis=1, tiled=True)  54.8 us
    all_gather x3, blocking collectives, apply_gram(): lax.all_gather(current, 'topic', axis=0, tiled=True)  39.5 us
    reduce_scatter x1, waiting for transfers between devices, per_device(): lax.psum_scatter(outer, 'term', scatter_dimension=1, tiled=True)  26.5 us
    reduce_scatter x1, waiting for transfers between devices, per_device(): lax.psum_scatter(contract_rows(row_block, row_block), 'topic', scatter_di...  23 us
    reduce_scatter x1, waiting for transfers between devices, per_device(): lax.psum_scatter(partial_data, 'term', scatter_dimension=1, tiled=True)  22.4 us
    all_gather x1, blocking collectives, per_device(): lax.all_gather(current, 'topic', axis=0, tiled=True)  13.1 us
    all_gather x1, blocking collectives, per_device(): code_row = lax.all_gather(current, 'term', axis=1, tiled=True)  8.61 us
  transfers between devices with their start and end apart: 4, of which 4 were waited for; matrix products, arithmetic and copies ran while one was open for 3% of the time, Pallas kernels for 0%

commit v1 on v0

--- a/solution.py
+++ b/solution.py
@@ -36,7 +36,7 @@
     gram_part = lax.psum_scatter(
         contract_rows(row_block, row_block), "topic", scatter_dimension=0, tiled=True
     )
-    gram_rows = lax.psum(gram_part, "term")
+    gram_rows = jnp.sum(lax.all_gather(gram_part, "term"), axis=0)
     current = codes
     for update in range(ITERS):
         current = current * data_share / (apply_gram(gram_rows, current) + EPSILON)

time: 285 us -> 258 us (0.905)
  waiting for transfers between devices: 129 us -> 99.8 us
    psum x1 -> x0, waiting for transfers between devices: 57 us -> none  [per_device(): gram_rows = lax.psum(gram_part, 'term')]
    reduce_scatter x1, waiting for transfers between devices: 22.4 us -> 35.3 us  [per_device(): lax.psum_scatter(partial_data, 'term', scatter_dimension=1, tiled=True)]
    all_gather x0 -> x1, waiting for transfers between devices: none -> 11.4 us  [per_device(): gram_rows = jnp.sum(lax.all_gather(gram_part, 'term'), axis=0)]
    reduce_scatter x1, waiting for transfers between devices: 23 us -> 26.6 us  [per_device(): lax.psum_scatter(contract_rows(row_block, row_block), 'topic', scatter_di...]
  transfers between devices with their start and end apart: 4 -> 4, of which waited for: 4 -> 4; matrix products, arithmetic and copies ran while one was open for 3% -> 4% of each run, Pallas kernels for 0% -> 0%
where the time goes in v1:
time: 258 us; the launch traced here: 257 us
  blocking collectives  117 us (45%)
  waiting for transfers between devices  99.8 us (39%)
  matrix products  18.3 us (7%)
  between operations  13.9 us (5%)
  local copies, waits for them, and re-layouts  5.32 us (2%)
  other arithmetic  3.2 us (1%)
    all_to_all x1, blocking collectives, per_device(): lax.all_to_all(factor, 'topic', split_axis=0, concat_axis=1, tiled=True)  54.8 us
    all_gather x3, blocking collectives, apply_gram(): lax.all_gather(current, 'topic', axis=0, tiled=True)  39.5 us
    reduce_scatter x1, waiting for transfers between devices, per_device(): lax.psum_scatter(partial_data, 'term', scatter_dimension=1, tiled=True)  35.3 us
    reduce_scatter x1, waiting for transfers between devices, per_device(): lax.psum_scatter(contract_rows(row_block, row_block), 'topic', scatter_di...  26.6 us
    reduce_scatter x1, waiting for transfers between devices, per_device(): lax.psum_scatter(outer, 'term', scatter_dimension=1, tiled=True)  26.5 us
    all_gather x1, blocking collectives, per_device(): lax.all_gather(current, 'topic', axis=0, tiled=True)  13.1 us
    all_gather x1, waiting for transfers between devices, per_device(): gram_rows = jnp.sum(lax.all_gather(gram_part, 'term'), axis=0)  11.4 us
    all_gather x1, blocking collectives, per_device(): code_row = lax.all_gather(current, 'term', axis=1, tiled=True)  9.2 us
  transfers between devices with their start and end apart: 4, of which 4 were waited for; matrix products, arithmetic and copies ran while one was open for 4% of the time, Pallas kernels for 0%

profile of v1, /device:TPU:0, one launch (start us, length us, event | category | flops | bytes accessed | tf_op | source)
XLA Modules:
  0.0 257.3 jit_solution(8143036711948958806)
XLA Ops:
  7.2 0.0 copy-start
  7.2 0.0 reduce-scatter.6.cloned.1.call-start
  7.2 54.8 %all_to_all.19 = bf16[4,2048,128]{2,1,0:T(8,128)(2,1)} all-to-all(bf16[4,2048,128]{2,1,0:T(8,128)(2,1)} %bitcast.22), channel_id=1, replica_groups=mesh['term'=8,'topic'=4] {'topic'}, dimensions={0} | all-to-all | bytes 4194304 | tf_op jit(solution)/shard_map/all_to_all | solution.py:35
  62.0 3.9 %copy.9 = bf16[2048,4,128]{0,2,1:T(8,128)(2,1)} copy(bf16[2048,4,128]{2,0,1:T(8,128)(2,1)} %bitcast.23) | data formatting | bytes 4194304 | tf_op jit(solution)/shard_map/all_to_all | solution.py:35
  66.0 0.0 copy-start.6
  66.0 4.5 %fusion.7 = f32[512,512]{1,0:T(8,128)} fusion(bf16[2048,512]{0,1:T(8,128)(2,1)} %bitcast.25), kind=kOutput, calls=%fused_computation.14 | convolution fusion | flops 1073741824 | bytes 3145728 | tf_op jit(solution)/shard_map/dot_general | solution.py:12
  70.4 0.0 reduce-scatter.6.cloned.1.call-update
  70.5 0.0 all-gather.3.cloned.1.call-start
  70.5 26.6 %reduce-scatter.6.cloned.1.call-done = f32[128,512]{1,0:T(8,128)} async-done(((f32[512,512]{1,0:T(8,128)}), f32[128,512]{1,0:T(8,128)}) %reduce-scatter.6.cloned.1.call-update) | async-done | bytes 262160 | tf_op jit(solution)/shard_map/reduce_scatter | solution.py:36
  97.1 0.0 all-gather.3.cloned.1.call-update
  97.2 0.0 reduce-scatter.4.cloned.1.call-start
  97.2 0.0 copy-done
  97.2 0.0 copy-done.6
  97.2 0.0 copy-start.2
  97.3 0.8 convolution_convert_fusion
  98.1 0.0 copy-start.1
  98.1 1.3 copy-done.1
  99.4 0.0 copy-done.2
  99.4 0.0 copy-start.5
  99.4 1.3 convolution_bitcast_fusion
  100.8 0.0 reduce-scatter.4.cloned.1.call-update
  100.8 0.0 reduce-scatter.8.cloned.1.call-start
  100.8 0.0 copy-done.5
  100.8 13.1 %all_gather.23 = f32[512,16]{0,1:T(8,128)S(1)} all-gather(f32[128,16]{0,1:T(8,128)S(1)} %copy-done.5), channel_id=1, replica_groups=mesh['term'=8,'topic'=4] {'topic'}, dimensions={0}, use_global_device_ids=true | all-gather | bytes 40960 | tf_op jit(solution)/shard_map/all_gather | solution.py:20
  114.0 11.4 %all-gather.3.cloned.1.call-done = f32[1024,512]{1,0:T(8,128)} async-done(((f32[128,512]{1,0:T(8,128)}), f32[1024,512]{1,0:T(8,128)}) %all-gather.3.cloned.1.call-update) | async-done | bytes 2097168 | tf_op jit(solution)/shard_map/all_gather | solution.py:39
  125.3 1.8 reduce_sum.9
  127.2 35.3 %reduce-scatter.4.cloned.1.call-done = f32[128,16]{0,1:T(8,128)} async-done(((f32[128,128]{0,1:T(8,128)}), f32[128,16]{0,1:T(8,128)}) %reduce-scatter.4.cloned.1.call-update) | async-done | bytes 8208 | tf_op jit(solution)/shard_map/reduce_scatter | solution.py:34
  162.5 1.0 fusion.3
  163.5 13.2 %all_gather.24 = f32[512,16]{0,1:T(8,128)S(1)} all-gather(f32[128,16]{0,1:T(8,128)S(1)} %fusion.3), channel_id=1, replica_groups=mesh['term'=8,'topic'=4] {'topic'}, dimensions={0}, use_global_device_ids=true | all-gather | bytes 40960 | tf_op jit(solution)/shard_map/all_gather | solution.py:20
  176.7 1.0 fusion.2
  177.7 13.1 %all_gather.25 = f32[512,16]{0,1:T(8,128)S(1)} all-gather(f32[128,16]{0,1:T(8,128)S(1)} %fusion.2), channel_id=1, replica_groups=mesh['term'=8,'topic'=4] {'topic'}, dimensions={0}, use_global_device_ids=true | all-gather | bytes 40960 | tf_op jit(solution)/shard_map/all_gather | solution.py:20
  190.8 1.0 fusion.1
  191.9 0.0 copy-start.3
  191.9 9.2 %all_gather.27 = f32[128,128]{0,1:T(8,128)S(1)} all-gather(f32[128,16]{0,1:T(8,128)S(1)} %fusion.1), channel_id=1, replica_groups=mesh['term'=8,'topic'=4] {'term'}, dimensions={1}, use_global_device_ids=true | all-gather | bytes 73728 | tf_op jit(solution)/shard_map/all_gather | solution.py:52
  201.1 13.1 %all_gather.26 = f32[512,16]{0,1:T(8,128)S(1)} all-gather(f32[128,16]{0,1:T(8,128)S(1)} %fusion.1), channel_id=1, replica_groups=mesh['term'=8,'topic'=4] {'topic'}, dimensions={0}, use_global_device_ids=true | all-gather | bytes 40960 | tf_op jit(solution)/shard_map/all_gather | solution.py:45
  214.2 1.3 fusion.8
  215.5 0.0 reduce-scatter.8.cloned.1.call-update
  215.5 0.0 copy-start.4
  215.6 7.4 %fusion = f32[8192,128]{1,0:T(8,128)} fusion(bf16[128,8192]{1,0:T(8,128)(2,1)} %copy-done.1, f32[128,128]{0,1:T(8,128)S(1)} %all_gather.27, f32[8192,128]{1,0:T(8,128)} %param.11), kind=kOutput, calls=%fused_computation.1 | convolution fusion | flops 1613758464 | bytes 10551296 | tf_op jit(solution)/shard_map/dot_general | solution.py:54
  222.9 0.0 copy-done.3
  222.9 26.5 %reduce-scatter.8.cloned.1.call-done = f32[128,64]{0,1:T(8,128)} async-done(((f32[128,512]{0,1:T(8,128)}), f32[128,64]{0,1:T(8,128)}) %reduce-scatter.8.cloned.1.call-update) | async-done | bytes 32784 | tf_op jit(solution)/shard_map/reduce_scatter | solution.py:50
  249.4 0.0 copy-done.4
  249.4 1.4 multiply_add_fusion
Async XLA Ops:
  7.2 90.1 %copy-start = (bf16[8192,128]{1,0:T(8,128)(2,1)S(1)}, bf16[8192,128]{1,0:T(8,128)(2,1)}, u32[]{:S(2)}) copy-start(bf16[8192,128]{1,0:T(8,128)(2,1)} %param.7) | copy-start | bytes 6291460
  7.2 90.0 %reduce-scatter.6.cloned.1.call-start = ((), (), s32[]{:S(2)}) async-start(), calls=%async_computation.5 | async-start | bytes 1310720 | tf_op jit(solution)/shard_map/reduce_scatter | solution.py:36
  66.0 31.3 %copy-start.6 = (s32[1,128]{1,0:T(1,128)S(1)}, s32[1,128]{1,0:T(1,128)}, u32[]{:S(2)}) copy-start(s32[1,128]{1,0:T(1,128)} %param.8) | copy-start | bytes 1540
  70.5 54.9 %all-gather.3.cloned.1.call-start = ((), (), s32[]{:S(2)}) async-start(), calls=%async_computation.7 | async-start | bytes 2359296 | tf_op jit(solution)/shard_map/all_gather | solution.py:39
  97.2 65.3 %reduce-scatter.4.cloned.1.call-start = ((), (), s32[]{:S(2)}) async-start(), calls=%async_computation.4 | async-start | bytes 73728 | tf_op jit(solution)/shard_map/reduce_scatter | solution.py:34
  97.2 2.2 copy-start.2
  98.1 1.3 copy-start.1
  99.4 1.4 copy-start.5
  100.8 148.6 %reduce-scatter.8.cloned.1.call-start = ((), (), s32[]{:S(2)}) async-start(), calls=%async_computation.6 | async-start | bytes 294912 | tf_op jit(solution)/shard_map/reduce_scatter | solution.py:50
  191.9 31.0 %copy-start.3 = (f32[128,16]{0,1:T(8,128)}, f32[128,16]{0,1:T(8,128)S(1)}, u32[]{:S(2)}) copy-start(f32[128,16]{0,1:T(8,128)S(1)} %fusion.1) | copy-start | bytes 24580
  215.5 33.8 %copy-start.4 = (f32[128,64]{0,1:T(8,128)S(1)}, f32[128,64]{0,1:T(8,128)}, u32[]{:S(2)}) copy-start(f32[128,64]{0,1:T(8,128)} %param.10) | copy-start | bytes 98308
Sparse Core Ops, SparseCore 0:
  70.6 26.5 reduce-scatter.5
  99.0 26.2 all-gather.2
  128.9 33.5 reduce-scatter.3
  215.7 33.6 reduce-scatter.7
